TPU v7x, 32 devices: a whole 2x2x4 slice. The times are simulated.
32 devices in a mesh: layer: 4 (over y, x), row: 2 (over core), col: 4 (over z).
Axes of the slice: x: 2, y: 2, z: 4, core: 2. Of those that a mesh axis runs over, the one named last changes fastest.
Arguments:
- cols: int32 [64, 16], P(('row', 'col'), 'layer'), may hold values from -1 to 63, as said below
- vals: bfloat16 [64, 16, 256, 256], P(('row', 'col'), 'layer'), as said below
- outcols: int32 [64, 4], P(('row', 'col')), may hold values from -1 to 63, as said below
Outputs:
- purified: bfloat16 [64, 4, 256, 256], P(('row', 'col'), 'layer')
Inputs may be any that keep to these rules, and one draw needn't show every extreme that they name: `cols`: slots 4 * l to 4 * l + 3 of block row i hold distinct block columns k with k mod 4 = l and |k - i| <= 6, or -1. Column i is always listed in row i, and k is listed in row i exactly when i is listed in row k. vals[i, s] is block (i, cols[i, s]) of a symmetric matrix: the block listed at (k, i) is the transpose of the one at (i, k). Slots holding -1 hold zeros. `outcols`: block row i lists distinct block columns j with i <= j <= i + 12, always i itself, or -1.
All inputs are finite; a program needn't handle non-finite values.
Results may differ from a plain program's by a relative error of at most 0.0085.
Values may be sent and summed in bfloat16 or wider, within the bound.
A program may use at most 64 MiB of HBM per device.

v0:
```python
import functools

import jax
import jax.numpy as jnp
from jax import lax
from jax.experimental import pallas as pl
from jax.experimental.pallas import tpu as pltpu
from jax.sharding import PartitionSpec as P

W = 6
MESH = pl.DeviceIdType.MESH


def kernel(
    sizes, cols_hbm, targets_hbm, vals_hbm, out_ref,
    cols_ref, targets_ref, vals_ref, pack, halo, right, part, own, kept, recv,
    load_sem, halo_send, halo_recv, forward_send, part_send, part_recv,
):
    rows, slots, outs, layers, groups, fine = sizes
    far = 2 * W
    steps = -(-(rows + W) // layers)
    layer = lax.axis_index("layer")
    group = lax.axis_index("row") * fine + lax.axis_index("col")
    base = group * rows
    zero_at = rows * slots
    halo_at = zero_at + 1

    def group_id(by):
        other = (group + by + groups) % groups
        return {"row": other // fine, "col": other % fine}

    def layer_id(by):
        return {"layer": (layer + by) % layers}

    def find(row, column):
        slot = jnp.int32(0)
        hit = jnp.int32(0)
        for s in range(slots):
            same = (cols_ref[row, s] == column).astype(jnp.int32)
            slot = slot + s * same
            hit = hit + same
        return jnp.minimum(slot, slots - 1), hit

    def halo_count(q):
        count = jnp.clip(q * layers + layer - rows + W + 1, 0, far)
        return jnp.where(q * layers + layer < rows + W, count, 0)

    def halo_copy(source, at, device):
        return pltpu.make_async_remote_copy(
            src_ref=pack.at[source], dst_ref=halo.at[at],
            send_sem=halo_send.at[source], recv_sem=halo_recv.at[at],
            device_id=device, device_id_type=MESH,
        )

    def forward_copy(source, at, to_layer):
        return pltpu.make_async_remote_copy(
            src_ref=halo.at[source], dst_ref=halo.at[at],
            send_sem=forward_send.at[source], recv_sem=halo_recv.at[at],
            device_id={"layer": to_layer}, device_id_type=MESH,
        )

    def mates(row):
        x, y = layer % 2, layer // 2
        flip_x, flip_y = y * 2 + 1 - x, (1 - y) * 2 + x
        even = row % 2 == 0
        both = (1 - y) * 2 + 1 - x
        return jnp.where(even, flip_x, flip_y), jnp.where(even, flip_y, flip_x), both

    def part_copy(at, to):
        return pltpu.make_async_remote_copy(
            src_ref=part.at[at], dst_ref=recv.at[at],
            send_sem=part_send.at[at], recv_sem=part_recv.at[at],
            device_id={"layer": to}, device_id_type=MESH,
        )

    loads = [
        pltpu.make_async_copy(cols_hbm, cols_ref, load_sem.at[0]),
        pltpu.make_async_copy(targets_hbm, targets_ref, load_sem.at[1]),
        pltpu.make_async_copy(vals_hbm, vals_ref, load_sem.at[2]),
    ]
    for load in loads:
        load.start()

    below = group_id(-1)
    neighbours = [group_id(-1), group_id(1)]
    neighbours += [layer_id(r) for r in range(1, layers)]
    for r in range(1, layers):
        neighbours += [group_id(-1) | layer_id(r), group_id(1) | layer_id(r)]
    barrier = pltpu.get_barrier_semaphore()
    for device in neighbours:
        pl.semaphore_signal(barrier, inc=1, device_id=device, device_id_type=MESH)
    for load in loads:
        load.wait()
    pl.semaphore_wait(barrier, len(neighbours))

    extra = steps * far

    def block_of(row, column):
        slot, hit = find(row, base + column)
        block = vals_ref[row, slot]
        return jnp.where(hit > 0, block, jnp.zeros_like(block))

    def straight(q, t):
        pack[q * far + t] = block_of(t, q * layers + layer - rows)
        halo_copy(q * far + t, q * far + t, below).start()

    def by_chip(t):
        return ((layer == layers - 2) & (t != layer)) | ((layer == layers - 1) & (t >= layers))

    def each_straight(act):
        def guarded(t, carry):
            @pl.when(by_chip(t))
            def _():
                act(1, t)
            return carry

        def plain(q):
            def body(t, carry):
                act(q, t)
                return carry
            return body

        lax.fori_loop(0, jnp.minimum(halo_count(0), rows), plain(0), 0)
        lax.fori_loop(0, jnp.minimum(halo_count(1), rows), guarded, 0)
        lax.fori_loop(0, jnp.minimum(halo_count(2), rows), plain(2), 0)
        lax.fori_loop(layers + layer, jnp.where(layer < 2, rows, layers + layer), plain(3), 0)

    def local_send(row):
        to = row - layers
        wanted = (layer != to) & (to != layers - 2) & ((to != 0) | (layer != layers - 1))
        return to, wanted

    for row in range(layers, 2 * layers):
        to, wanted = local_send(row)

        @pl.when(layer == to)
        def _(row=row):
            right[halo_at + far + layer] = block_of(row, rows + layer).T

        @pl.when(wanted)
        def _(row=row, to=to):
            pack[extra + to] = block_of(row, rows + layer).T
            halo_copy(extra + to, far + layer, {"layer": jnp.int32(to)}).start()

    def upper_copy(inner):
        to = inner % layers
        q = (rows + inner) // layers
        return halo_copy(
            extra + layers + inner, q * far + rows + layer, below | {"layer": to}
        )

    def upper_send(inner, carry):
        pack[extra + layers + inner] = block_of(inner, rows + layer).T
        upper_copy(inner).start()
        return carry

    each_straight(straight)
    lax.fori_loop(rows - W + layer, W, upper_send, 0)

    right[zero_at] = jnp.zeros(right.shape[1:], right.dtype)

    def keep(n, carry):
        right[n] = vals_ref[n // slots, n % slots]
        return carry

    lax.fori_loop(0, rows * slots, keep, 0)

    def product(row, o):
        target = targets_ref[row, o]
        there = target - base
        near = jnp.clip(there, 0, rows - 1)
        total = None
        for s in range(slots):
            column = cols_ref[row, s]
            slot, hit = find(near, column)
            local_at = jnp.where(hit > 0, near * slots + slot, zero_at)
            t = there - rows
            place = column - base
            q = (place - layer) // layers
            reach = (place >= t + rows - W) & (t < far)
            far_at = jnp.where(reach, halo_at + q * far + t, zero_at)
            at = jnp.where(there < rows, local_at, far_at)
            at = jnp.where((target >= 0) & (column >= 0), at, zero_at)
            at = jnp.clip(at, 0, right.shape[0] - 1)
            term = lax.dot_general(
                vals_ref[row, s], right[at], (((1,), (1,)), ((), ())),
                preferred_element_type=jnp.float32,
            )
            total = term if total is None else total + term
        slot, hit = find(row, target)
        mine = (hit > 0) & (target >= 0)
        block = vals_ref[row, jnp.where(mine, slot, 0)].astype(jnp.float32)
        twice = jnp.where(mine, 2.0 * block, jnp.zeros_like(block))
        return twice - total

    def one_row(row, carry):
        first, second, both = mates(row)
        part[2 * row + 1] = product(row, both).astype(part.dtype)
        part_copy(2 * row + 1, first).start()
        part[2 * row] = product(row, first).astype(part.dtype)
        part_copy(2 * row, first).start()
        kept[row] = product(row, second)
        own[row] = product(row, layer)
        return carry

    def relay(row, carry):
        first, second, _ = mates(row)
        part_copy(2 * row + 1, first).wait_recv()
        total = kept[row] + recv[2 * row + 1].astype(jnp.float32)
        part[2 * rows + row] = total.astype(part.dtype)
        part_copy(2 * rows + row, second).start()
        return carry

    def forwarded(q, t):
        to = t - layers
        return to, (t >= layers) & (t < layers + 2) & (to != layer) & (to + layers > layers * (q - 2) + layer)

    for q in range(steps):
        count = halo_count(q)

        def arrive(t, carry, q=q):
            at = q * far + t
            if q == 1:
                comes = t != layer
            elif q == 3:
                comes = (t >= layers + layer) | (t % layers != layer)
            else:
                comes = t >= 0

            @pl.when(comes)
            def _():
                halo_copy(at, at, below).wait_recv()
                if q == 3:
                    @pl.when(t < layers + layer)
                    def _():
                        right[halo_at + at] = halo[at].T

                    @pl.when(t >= layers + layer)
                    def _():
                        right[halo_at + at] = halo[at]
                else:
                    right[halo_at + at] = halo[at]
            if q >= 2:
                to, wanted = forwarded(q, t)

                @pl.when(wanted)
                def _():
                    forward_copy(at, 3 * far + (q - 2) * layers + layer, to).start()
            if q == 2:
                @pl.when((t == 2) | (t == 3))
                def _():
                    relay(t - 2, 0)

                @pl.when((layer >= 2) & ((t == 6) | (t == 7)))
                def _():
                    relay(t - 4, 0)

                @pl.when((t == layers + layer) & (layer < 2))
                def _():
                    right[halo_at + 3 * far + layer] = halo[at].T
            return carry

        lax.fori_loop(0, count, arrive, 0)
        first = jnp.clip(q * layers + layer - W, 0, rows) if q else 0
        last = jnp.clip((q + 1) * layers + layer - W, 0, rows) if q < steps - 1 else rows
        lax.fori_loop(first, last, one_row, 0)
        if q >= 2:
            start, middle = jnp.where(layer >= 2, 4, 2), jnp.where(layer >= 2, W, W - 1)
            lax.fori_loop(start if q == 2 else middle, middle if q == 2 else rows, relay, 0)

    def finish(row, carry):
        first, second, _ = mates(row)
        part_copy(2 * row, first).wait_recv()
        part_copy(2 * rows + row, second).wait_recv()
        total = own[row] + recv[2 * row].astype(jnp.float32)
        total = total + recv[2 * rows + row].astype(jnp.float32)
        out_ref[row, 0] = total.astype(out_ref.dtype)
        return carry

    lax.fori_loop(0, rows, finish, 0)

    each_straight(lambda q, t: halo_copy(q * far + t, q * far + t, below).wait_send())

    for row in range(layers, 2 * layers):
        to, wanted = local_send(row)

        @pl.when(wanted)
        def _(to=to):
            halo_copy(extra + to, far + layer, {"layer": jnp.int32(to)}).wait_send()

    def upper_done(inner, carry):
        upper_copy(inner).wait_send()
        return carry

    lax.fori_loop(rows - W + layer, W, upper_done, 0)

    for q in (2, 3):
        def forward_done(t, carry, q=q):
            to, wanted = forwarded(q, t)

            @pl.when(wanted)
            def _():
                forward_copy(q * far + t, 3 * far + (q - 2) * layers + layer, to).wait_send()
            return carry

        lax.fori_loop(0, halo_count(q), forward_done, 0)
    def part_done(row, carry):
        first, second, _ = mates(row)
        part_copy(2 * row, first).wait_send()
        part_copy(2 * row + 1, first).wait_send()
        part_copy(2 * rows + row, second).wait_send()
        return carry

    lax.fori_loop(0, rows, part_done, 0)


def solution(mesh):
    layers = mesh.shape["layer"]
    fine = mesh.shape["col"]
    groups = mesh.shape["row"] * fine

    def per_device(cols, vals, outcols):
        rows, slots, size, _ = vals.shape
        outs = outcols.shape[1]
        assert rows == 2 * layers and rows == W + 2 and layers == 4
        far = 2 * W
        steps = -(-(rows + W) // layers)
        block = (size, size)
        sent = (layers - 1) * rows
        return pl.pallas_call(
            functools.partial(kernel, (rows, slots, outs, layers, groups, fine)),
            out_shape=jax.ShapeDtypeStruct((rows, outs // layers) + block, jnp.bfloat16),
            in_specs=[
                pl.BlockSpec(memory_space=pl.ANY),
                pl.BlockSpec(memory_space=pl.ANY),
                pl.BlockSpec(memory_space=pl.ANY),
            ],
            out_specs=pl.BlockSpec(memory_space=pltpu.VMEM),
            scratch_shapes=[
                pltpu.SMEM(cols.shape, cols.dtype),
                pltpu.SMEM(outcols.shape, outcols.dtype),
                pltpu.VMEM(vals.shape, vals.dtype),
                pltpu.VMEM((steps * far + layers + rows,) + block, jnp.bfloat16),
                pltpu.VMEM((steps * far,) + block, jnp.bfloat16),
                pltpu.VMEM((rows * slots + 1 + steps * far,) + block, jnp.bfloat16),
                pltpu.VMEM((sent,) + block, jnp.bfloat16),
                pltpu.VMEM((rows,) + block, jnp.float32),
                pltpu.VMEM((rows,) + block, jnp.float32),
                pltpu.VMEM((sent,) + block, jnp.bfloat16),
                pltpu.SemaphoreType.DMA((3,)),
                pltpu.SemaphoreType.DMA((steps * far + layers + rows,)),
                pltpu.SemaphoreType.DMA((steps * far,)),
                pltpu.SemaphoreType.DMA((steps * far,)),
                pltpu.SemaphoreType.DMA((sent,)),
                pltpu.SemaphoreType.DMA((sent,)),
            ],
            compiler_params=pltpu.CompilerParams(collective_id=0, has_side_effects=True),
        )(cols, outcols, vals)

    in_specs = (
        P(("row", "col"), "layer"),
        P(("row", "col"), "layer", None, None),
        P(("row", "col"), None),
    )
    return jax.shard_map(
        per_device, mesh=mesh, in_specs=in_specs,
        out_specs=P(("row", "col"), "layer", None, None), check_vma=False,
    )
```

profile of v0, /device:TPU:0, one launch (start us, length us, event | category | flops | bytes accessed | tf_op | source)
XLA Modules:
  0.0 75.6 jit_solution(1037375859419917482)
XLA Ops:
  0.0 1.3 %copy.4.cols_hbm = s32[8,4]{1,0:T(8,128)} copy(s32[8,4]{0,1:T(4,128)} %param.3) | data formatting | bytes 256 | tf_op args[0]
  1.3 1.3 %copy.5.targets_hbm = s32[8,4]{1,0:T(8,128)} copy(s32[8,4]{0,1:T(4,128)} %param.5) | data formatting | bytes 256 | tf_op args[2]
  2.7 70.6 %shard_map.37 = bf16[8,1,256,256]{3,2,1,0:T(8,128)(2,1)} custom-call(s32[8,4]{1,0:T(8,128)} %copy.4.cols_hbm, s32[8,4]{1,0:T(8,128)} %copy.5.targets_hbm, bf16[8,4,256,256]{3,2,1,0:T(8,128)(2,1)} %vals_hbm.1), custom_call_target="tpu_custom_call" | custom-call | tf_op jit(solution)/shard_map/pallas_call | solution.py:330
  73.3 2.3 %copy.7 = bf16[8,1,256,256]{3,2,1,0:T(8,128)(2,1)} copy(bf16[8,1,256,256]{3,2,1,0:T(8,128)(2,1)} %shard_map.37) | data formatting | bytes 2097152
where the time goes:
time: 76.3 us; the launch traced here: 75.6 us
  Pallas kernels  70.6 us (93%)
  local copies, waits for them, and re-layouts  4.95 us (6%)
    pallas_call x1, Pallas kernels, per_device(): pl.pallas_call(functools.partial(kernel, (rows, slots, outs, layers, grou...  70.6 us
    unnamed x3, local copies, waits for them, and re-layouts  4.95 us

commit v1 on v0

v1 whole, which is shorter than its diff:
```python
import functools

import jax
import jax.numpy as jnp
from jax import lax
from jax.experimental import pallas as pl
from jax.experimental.pallas import tpu as pltpu
from jax.sharding import PartitionSpec as P

W = 6
MESH = pl.DeviceIdType.MESH

LOCAL = (
    ((3, 0), (2, 0), (5, 0), (6, 0), (6, 4), (7, 0), (7, 4)),
    ((3, 1), (4, 1), (6, 1), (7, 1), (7, 5)),
    ((4, 2), (5, 2), (7, 2)),
    ((5, 3), (6, 3)),
)
LOCAL_BELOW = ()
FORWARD = ((1, 0), (2, 0), (3, 1), (3, 2))
X_FIRST = (True, False, True, False, True, False, True, False)


def kernel(
    sizes, cols_hbm, targets_hbm, vals_hbm, out_ref,
    cols_ref, targets_ref, targets_up, right, pack, halo, lent, terms_out, terms_in,
    part, own, kept, recv,
    load_sem, pack_send, halo_recv, forward_send, lent_send, lent_recv, target_send, target_recv,
    term_send, term_recv, part_send, part_recv,
):
    rows, slots, outs, layers, groups, fine = sizes
    far = 2 * W
    layer = lax.axis_index("layer")
    group = lax.axis_index("row") * fine + lax.axis_index("col")
    base = group * rows
    zero_at = rows * slots
    halo_at = zero_at + 1
    has_above = group < groups - 1
    has_below = group > 0

    def group_id(by):
        other = (group + by + groups) % groups
        return {"row": other // fine, "col": other % fine}

    below, above = group_id(-1), group_id(1)

    def sel(values):
        if len(set(values)) == 1:
            return jnp.int32(values[0])
        out = jnp.int32(values[-1])
        for n in range(len(values) - 1):
            out = jnp.where(layer == n, values[n], out)
        return out

    def among(which):
        which = sorted(set(which))
        if len(which) == layers:
            return None
        cond = layer == which[0]
        for n in which[1:]:
            cond = cond | (layer == n)
        return cond

    def guard(which, *more):
        conds = [c for c in (among(which), *more) if c is not None]
        def wrap(f):
            if not conds:
                f()
                return
            cond = conds[0]
            for c in conds[1:]:
                cond = cond & c
            pl.when(cond)(f)
        return wrap

    def find(row, column):
        slot = jnp.int32(0)
        hit = jnp.int32(0)
        for s in range(slots):
            same = (cols_ref[s, row] == column).astype(jnp.int32)
            slot = slot + s * same
            hit = hit + same
        return jnp.minimum(slot, slots - 1), hit

    def block_of(row, column):
        slot, hit = find(row, base + column)
        block = right[row * slots + slot]
        return jnp.where(hit > 0, block, jnp.zeros_like(block))

    lists = [[] for _ in range(layers)]
    for k, t in LOCAL_BELOW:
        lists[k % layers].append((k, t))
    forwarded = {(rows + b, a) for a, b in FORWARD}
    for n in range(layers):
        k = rows + n
        mine = [(k, t) for t in range(min(k - rows + W + 1, rows)) if (k, t) not in forwarded]
        early = [(rows + a, b) for a, b in FORWARD if a == n]
        lists[n] += early + [e for e in mine if e not in early]
    crossing = [[e for e in LOCAL[n] if e not in LOCAL_BELOW] for n in range(layers)]
    down_most = max(len(x) for x in lists)
    cross_most = max(len(x) for x in crossing)
    lent_at = down_most + cross_most

    def at_of(k, t):
        return k // layers * far + t

    def down_copy(n):
        at = sel([at_of(*x[n]) if n < len(x) else 0 for x in lists])
        return pltpu.make_async_remote_copy(
            src_ref=pack.at[n], dst_ref=halo.at[at], send_sem=pack_send.at[n], recv_sem=halo_recv.at[at],
            device_id=below, device_id_type=MESH,
        )

    def down_has(n):
        return [m for m in range(layers) if n < len(lists[m])]

    def cross_copy(n):
        at = sel([at_of(*x[n]) if n < len(x) else 0 for x in crossing])
        to = sel([x[n][0] % layers if n < len(x) else 0 for x in crossing])
        return pltpu.make_async_remote_copy(
            src_ref=pack.at[down_most + n], dst_ref=halo.at[at],
            send_sem=pack_send.at[down_most + n], recv_sem=halo_recv.at[at],
            device_id={"layer": to}, device_id_type=MESH,
        )

    def cross_has(n):
        return [m for m in range(layers) if n < len(crossing[m])]

    def lent_copy(i):
        return pltpu.make_async_remote_copy(
            src_ref=pack.at[lent_at + i], dst_ref=lent.at[i], send_sem=lent_send.at[i], recv_sem=lent_recv.at[i],
            device_id=above, device_id_type=MESH,
        )

    def target_copy():
        return pltpu.make_async_remote_copy(
            src_ref=targets_ref, dst_ref=targets_up, send_sem=target_send, recv_sem=target_recv,
            device_id=above, device_id_type=MESH,
        )

    def forward_copy(n):
        a, b = FORWARD[n]
        return pltpu.make_async_remote_copy(
            src_ref=halo.at[at_of(rows + a, b)], dst_ref=halo.at[at_of(rows + b, a)],
            send_sem=forward_send.at[n], recv_sem=halo_recv.at[at_of(rows + b, a)],
            device_id={"layer": jnp.int32(b)}, device_id_type=MESH,
        )

    passed = [(k, t) for k in range(layers) for t in range(k - rows + W + 1)]

    def pass_copy(n):
        k, t = passed[n]
        return pltpu.make_async_remote_copy(
            src_ref=halo.at[at_of(k, t)], dst_ref=halo.at[at_of(rows + k, rows + t)],
            send_sem=forward_send.at[len(FORWARD) + n], recv_sem=halo_recv.at[at_of(rows + k, rows + t)],
            device_id=below, device_id_type=MESH,
        )

    def term_copy(n):
        return pltpu.make_async_remote_copy(
            src_ref=terms_out.at[n], dst_ref=terms_in.at[n], send_sem=term_send.at[n], recv_sem=term_recv.at[n],
            device_id=below, device_id_type=MESH,
        )

    def part_copy(at, to):
        return pltpu.make_async_remote_copy(
            src_ref=part.at[at], dst_ref=recv.at[at], send_sem=part_send.at[at], recv_sem=part_recv.at[at],
            device_id={"layer": to}, device_id_type=MESH,
        )

    lx, ly = layer % 2, layer // 2
    flip_x, flip_y, both = ly * 2 + 1 - lx, (1 - ly) * 2 + lx, (1 - ly) * 2 + 1 - lx

    def mates(row):
        return (flip_x, flip_y) if X_FIRST[row] else (flip_y, flip_x)

    loads = [
        pltpu.make_async_copy(cols_hbm, cols_ref, load_sem.at[0]),
        pltpu.make_async_copy(targets_hbm, targets_ref, load_sem.at[1]),
        pltpu.make_async_copy(vals_hbm, right.at[pl.ds(0, rows * slots)], load_sem.at[2]),
    ]
    for load in loads:
        load.start()
    barrier = pltpu.get_barrier_semaphore()
    for r in range(1, layers):
        to = {"layer": (layer + r) % layers}
        pl.semaphore_signal(barrier, inc=1, device_id=to, device_id_type=MESH)

    @pl.when(has_below)
    def _():
        pl.semaphore_signal(barrier, inc=1, device_id=below, device_id_type=MESH)

    @pl.when(has_above)
    def _():
        pl.semaphore_signal(barrier, inc=1, device_id=above, device_id_type=MESH)

    right[zero_at] = jnp.zeros(right.shape[1:], right.dtype)
    for load in loads:
        load.wait()

    def cross_pack(n):
        @guard(cross_has(n), has_above)
        def _():
            row = sel([x[n][0] if n < len(x) else 0 for x in crossing])
            t = sel([x[n][1] if n < len(x) else 0 for x in crossing])
            pack[down_most + n] = block_of(row, rows + t).T

    def cross_start(n):
        @guard(cross_has(n), has_above)
        def _():
            cross_copy(n).start()

    def down_pack(n):
        @guard(down_has(n), has_below)
        def _():
            k = sel([x[n][0] if n < len(x) else 0 for x in lists])
            t = sel([x[n][1] if n < len(x) else 0 for x in lists])
            pack[n] = block_of(t, k - rows)

    def down_start(n):
        @guard(down_has(n), has_below)
        def _():
            down_copy(n).start()

    cross_pack(0)
    down_pack(0)
    pl.semaphore_wait(barrier, layers - 1 + has_below.astype(jnp.int32) + has_above.astype(jnp.int32))
    cross_start(0)
    down_start(0)

    @pl.when(has_above & (layer < 2))
    def _():
        target_copy().start()
        for i in range(2):
            @guard((0,) if i == 0 else (0, 1))
            def _(i=i):
                pack[lent_at + i] = block_of(W + i, rows + layers + layer)
                lent_copy(i).start()

    for n in range(1, max(down_most, cross_most)):
        if n < cross_most:
            cross_pack(n)
            cross_start(n)
        if n < down_most:
            down_pack(n)
            down_start(n)

    right[halo_at + far + layer] = block_of(layers + layer, rows + layer).T

    def arrive(k, t):
        @guard((k % layers,), group < groups - 2 if t >= rows else has_above)
        def _():
            at = at_of(k, t)
            pltpu.make_async_remote_copy(
                src_ref=halo.at[at], dst_ref=halo.at[at], send_sem=pack_send.at[0], recv_sem=halo_recv.at[at],
                device_id=below, device_id_type=MESH,
            ).wait_recv()
            block = halo[at]
            right[halo_at + at] = block.T if (k, t) in forwarded else block
            for n, (a, b) in enumerate(FORWARD):
                if (rows + a, b) == (k, t):
                    forward_copy(n).start()
            if (k, t) in passed:
                @pl.when(has_below)
                def _():
                    pass_copy(passed.index((k, t))).start()

    def product(row, o):
        target = targets_ref[o, row]
        there = target - base
        near = jnp.clip(there, 0, rows - 1)
        t = there - rows
        total = None
        for s in range(slots):
            column = cols_ref[s, row]
            slot, hit = find(near, column)
            local_at = jnp.where(hit > 0, near * slots + slot, zero_at)
            place = column - base
            q = (place - layer) // layers
            reach = (place >= t + rows - W) & (place < rows + layers) & (t < far)
            far_at = jnp.where(reach, halo_at + q * far + t, zero_at)
            at = jnp.where(there < rows, local_at, far_at)
            at = jnp.where((target >= 0) & (column >= 0), at, zero_at)
            at = jnp.clip(at, 0, right.shape[0] - 1)
            term = lax.dot_general(
                right[row * slots + s], right[at], (((1,), (1,)), ((), ())),
                preferred_element_type=jnp.float32,
            )
            total = term if total is None else total + term
        if row >= W:
            lends = ((layer == 0) | ((layer == 1) & (row > W))) & has_above
            theirs = terms_in[(row - W) * outs + o].astype(jnp.float32)
            total = total + jnp.where(lends, theirs, jnp.zeros_like(theirs))
        slot, hit = find(row, target)
        mine = (hit > 0) & (target >= 0)
        block = right[row * slots + jnp.where(mine, slot, 0)].astype(jnp.float32)
        twice = jnp.where(mine, 2.0 * block, jnp.zeros_like(block))
        return twice - total

    def terms(i):
        def body(o, carry):
            target = targets_up[o, W + i]
            there = target - base
            near = jnp.clip(there, 0, rows - 1)
            slot, hit = find(near, base + layers + layer)
            local_at = jnp.where(hit > 0, near * slots + slot, zero_at)
            t = there - rows
            reach = layers + layer >= t + rows - W
            far_at = jnp.where(reach, halo_at + far + t, zero_at)
            at = jnp.where(there < rows, local_at, far_at)
            at = jnp.where((target >= 0) & (there >= 0), at, zero_at)
            at = jnp.clip(at, 0, right.shape[0] - 1)
            term = lax.dot_general(
                lent[i], right[at], (((1,), (1,)), ((), ())), preferred_element_type=jnp.float32,
            )
            terms_out[i * outs + o] = term.astype(terms_out.dtype)
            term_copy(i * outs + o).start()
            return carry
        lax.fori_loop(0, outs, body, 0)

    def one_row(row):
        first, second = mates(row)
        part[2 * row + 1] = product(row, both).astype(part.dtype)
        part_copy(2 * row + 1, first).start()
        part[2 * row] = product(row, first).astype(part.dtype)
        part_copy(2 * row, first).start()
        kept[row] = product(row, second)
        own[row] = product(row, layer)

    def relay(row):
        first, second = mates(row)
        part_copy(2 * row + 1, first).wait_recv()
        total = kept[row] + recv[2 * row + 1].astype(jnp.float32)
        part[2 * rows + row] = total.astype(part.dtype)
        part_copy(2 * rows + row, second).start()

    needs = [[] for _ in range(rows + 2)]
    for q in range(2):
        for n in range(layers):
            k = q * layers + n
            for t in range(max(0, k - rows + W + 1)):
                if (t % layers) != n:
                    needs[0 if k < rows - 1 and t < far - rows + 1 else 1].append((k, t))
    fore = [(rows + a, b) for a, b in FORWARD]
    needs[1] += fore
    for n in range(layers):
        k = rows + n
        rest = [e for e in lists[n] if e[0] == k and e not in fore]
        rest += [e for e in sorted(forwarded) if e[0] == k]
        rest += [(k, t) for t in range(rows, k - rows + W + 1)]
        needs[2 + n] += rest

    relay_at = [[min(row + 2, rows) if row != 1 + n else 2 + n for row in range(rows)] for n in range(layers)]

    for row in range(rows):
        for at_row in range(rows):
            which = [n for n in range(layers) if relay_at[n][at_row] == row]
            if which:
                guard(which)(functools.partial(relay, at_row))
        if row == 2:
            @pl.when(has_below & (layer < 2))
            def _():
                target_copy().wait_recv()
                for i in range(2):
                    @guard((0,) if i == 0 else (0, 1))
                    def _(i=i):
                        lent_copy(i).wait_recv()
                        terms(i)
        for k, t in needs[row]:
            arrive(k, t)
        if row >= W:
            @guard((0,) if row == W else (0, 1), has_above)
            def _(row=row):
                for o in range(outs):
                    term_copy((row - W) * outs + o).wait_recv()
        one_row(row)
    for at_row in range(rows):
        which = [n for n in range(layers) if relay_at[n][at_row] >= rows]
        if which:
            guard(which)(functools.partial(relay, at_row))

    for row in range(rows):
        first, second = mates(row)
        part_copy(2 * row, first).wait_recv()
        part_copy(2 * rows + row, second).wait_recv()
        total = own[row] + recv[2 * row].astype(jnp.float32)
        total = total + recv[2 * rows + row].astype(jnp.float32)
        out_ref[row, 0] = total.astype(out_ref.dtype)

    for n in range(cross_most):
        guard(cross_has(n), has_above)(lambda n=n: cross_copy(n).wait_send())
    for n in range(down_most):
        guard(down_has(n), has_below)(lambda n=n: down_copy(n).wait_send())
    for n, (a, b) in enumerate(FORWARD):
        guard((a,), has_above)(lambda n=n: forward_copy(n).wait_send())
    for n, (k, t) in enumerate(passed):
        guard((k,), has_below, has_above)(lambda n=n: pass_copy(n).wait_send())

    @pl.when(has_above & (layer < 2))
    def _():
        target_copy().wait_send()
        for i in range(2):
            guard((0,) if i == 0 else (0, 1))(lambda i=i: lent_copy(i).wait_send())

    @pl.when(has_below & (layer < 2))
    def _():
        for i in range(2):
            @guard((0,) if i == 0 else (0, 1))
            def _(i=i):
                for o in range(outs):
                    term_copy(i * outs + o).wait_send()

    for row in range(rows):
        first, second = mates(row)
        part_copy(2 * row, first).wait_send()
        part_copy(2 * row + 1, first).wait_send()
        part_copy(2 * rows + row, second).wait_send()


def solution(mesh):
    layers = mesh.shape["layer"]
    fine = mesh.shape["col"]
    groups = mesh.shape["row"] * fine

    def per_device(cols, vals, outcols):
        rows, slots, size, _ = vals.shape
        outs = outcols.shape[1]
        assert rows == 2 * layers and rows == W + 2 and layers == 4 and outs == layers
        far = 2 * W
        block = (size, size)
        halo = 3 * far
        sent = 3 * rows
        packs = 20
        return pl.pallas_call(
            functools.partial(kernel, (rows, slots, outs, layers, groups, fine)),
            out_shape=jax.ShapeDtypeStruct((rows, outs // layers) + block, jnp.bfloat16),
            in_specs=[
                pl.BlockSpec(memory_space=pl.ANY),
                pl.BlockSpec(memory_space=pl.ANY),
                pl.BlockSpec(memory_space=pl.ANY),
            ],
            out_specs=pl.BlockSpec(memory_space=pltpu.VMEM),
            scratch_shapes=[
                pltpu.SMEM(cols.shape[::-1], cols.dtype),
                pltpu.SMEM(outcols.shape[::-1], outcols.dtype),
                pltpu.SMEM(outcols.shape[::-1], outcols.dtype),
                pltpu.VMEM((rows * slots + 1 + halo,) + block, jnp.bfloat16),
                pltpu.VMEM((packs,) + block, jnp.bfloat16),
                pltpu.VMEM((halo,) + block, jnp.bfloat16),
                pltpu.VMEM((2,) + block, jnp.bfloat16),
                pltpu.VMEM((2 * outs,) + block, jnp.bfloat16),
                pltpu.VMEM((2 * outs,) + block, jnp.bfloat16),
                pltpu.VMEM((sent,) + block, jnp.bfloat16),
                pltpu.VMEM((rows,) + block, jnp.float32),
                pltpu.VMEM((rows,) + block, jnp.float32),
                pltpu.VMEM((sent,) + block, jnp.bfloat16),
                pltpu.SemaphoreType.DMA((3,)),
                pltpu.SemaphoreType.DMA((packs,)),
                pltpu.SemaphoreType.DMA((halo,)),
                pltpu.SemaphoreType.DMA((12,)),
                pltpu.SemaphoreType.DMA((2,)),
                pltpu.SemaphoreType.DMA((2,)),
                pltpu.SemaphoreType.DMA,
                pltpu.SemaphoreType.DMA,
                pltpu.SemaphoreType.DMA((2 * outs,)),
                pltpu.SemaphoreType.DMA((2 * outs,)),
                pltpu.SemaphoreType.DMA((sent,)),
                pltpu.SemaphoreType.DMA((sent,)),
            ],
            compiler_params=pltpu.CompilerParams(collective_id=0, has_side_effects=True),
        )(cols.T, outcols.T, vals.reshape((rows * slots,) + block))

    in_specs = (
        P(("row", "col"), "layer"),
        P(("row", "col"), "layer", None, None),
        P(("row", "col"), None),
    )
    return jax.shard_map(
        per_device, mesh=mesh, in_specs=in_specs,
        out_specs=P(("row", "col"), "layer", None, None), check_vma=False,
    )
```

time: 76.3 us -> 66.3 us (0.87)
  Pallas kernels: 70.6 us -> 63.9 us
  local copies, waits for them, and re-layouts: 4.95 us -> 2.26 us
    pallas_call x1, Pallas kernels: 70.6 us -> 63.9 us  [per_device(): pl.pallas_call(functools.partial(kernel, (rows, slots, outs, layers, grou...]
    unnamed x3 -> x1, local copies, waits for them, and re-layouts: 4.95 us -> 2.26 us
where the time goes in v1:
time: 66.3 us; the launch traced here: 66.1 us
  Pallas kernels  63.9 us (96%)
  local copies, waits for them, and re-layouts  2.26 us (3%)
    pallas_call x1, Pallas kernels, per_device(): pl.pallas_call(functools.partial(kernel, (rows, slots, outs, layers, grou...  63.9 us
    unnamed x1, local copies, waits for them, and re-layouts  2.26 us

profile of v1, /device:TPU:0, one launch (start us, length us, event | category | flops | bytes accessed | tf_op | source)
XLA Modules:
  0.0 66.1 jit_solution(2983133977751443433)
XLA Ops:
  0.0 63.9 %shard_map.37 = bf16[8,1,256,256]{3,2,1,0:T(8,128)(2,1)} custom-call(s32[4,8]{1,0:T(4,128)} %bitcast.4, s32[4,8]{1,0:T(4,128)} %bitcast.5, bf16[32,256,256]{2,1,0:T(8,128)(2,1)} %bitcast.3), custom_call_target="tpu_custom_call" | custom-call | tf_op jit(solution)/shard_map/pallas_call | solution.py:434
  63.9 2.3 %copy.5 = bf16[8,1,256,256]{3,2,1,0:T(8,128)(2,1)} copy(bf16[8,1,256,256]{3,2,1,0:T(8,128)(2,1)} %shard_map.37) | data formatting | bytes 2097152

commit v2 on v1

--- a/solution.py
+++ b/solution.py
@@ -10,15 +10,76 @@
 W = 6
 MESH = pl.DeviceIdType.MESH
 
+FAR_LEND, FAR_TERMS = 2, 4
 LOCAL = (
-    ((3, 0), (2, 0), (5, 0), (6, 0), (6, 4), (7, 0), (7, 4)),
-    ((3, 1), (4, 1), (6, 1), (7, 1), (7, 5)),
-    ((4, 2), (5, 2), (7, 2)),
+    ((2, 0), (6, 0), (7, 0), (5, 0)),
+    ((7, 5), (4, 1), (6, 1), (3, 1), (7, 1)),
+    ((5, 2), (7, 2), (4, 2)),
     ((5, 3), (6, 3)),
 )
-LOCAL_BELOW = ()
-FORWARD = ((1, 0), (2, 0), (3, 1), (3, 2))
-X_FIRST = (True, False, True, False, True, False, True, False)
+BELOW = (
+    ((8, 5), (8, 1), (8, 0), (8, 4), (8, 6)),
+    ((9, 2), (9, 6), (9, 1), (9, 7), (9, 5), (9, 4), (9, 3)),
+    ((10, 3), (6, 4), (10, 0), (10, 6), (10, 5), (10, 4), (10, 2), (10, 7)),
+    ((11, 0), (3, 0), (11, 5), (7, 4), (11, 6), (11, 7), (11, 4), (11, 3)),
+)
+FORWARD = ((2, 0), (1, 3), (1, 2), (3, 0), (0, 1), (2, 3))
+OVER_Y = (
+    (0, 0, 1, 0),
+    (0, 1, 0, 0),
+    (1, 0, 1, 0),
+    (0, 0, 0, 1),
+    (1, 0, 1, 1),
+    (0, 1, 0, 0),
+    (1, 0, 1, 1),
+    (1, 1, 0, 0),
+)
+STEPS = (
+    (
+        (('A', 8, 5), ('A', 4, 1), ('A', 4, 2)),
+        (),
+        (('A', 8, 1), ('T', 0, 0), ('A', 8, 0), ('A', 8, 3), ('A', 8, 4), ('R', 0, 0), ('A', 8, 2), ('A', 8, 6)),
+        (),
+        (),
+        (('R', 0, 1),),
+        (('R', 2, 0), ('R', 2, 1)),
+        (('R', 3, 0), ('R', 4, 0), ('R', 4, 1)),
+        (('R', 6, 0), ('R', 6, 1)),
+    ),
+    (
+        (('A', 5, 3), ('A', 9, 2), ('A', 5, 2), ('A', 9, 6), ('A', 5, 0)),
+        (),
+        (('A', 9, 1), ('R', 0, 0), ('T', 0, 0)),
+        (('A', 9, 7), ('R', 1, 0), ('A', 9, 5), ('A', 9, 4), ('A', 9, 0), ('A', 9, 3)),
+        (),
+        (),
+        (('R', 3, 0), ('R', 3, 1)),
+        (('R', 4, 1), ('R', 5, 0)),
+        (('R', 6, 1),),
+    ),
+    (
+        (('A', 2, 0), ('A', 10, 3), ('A', 6, 3), ('A', 6, 0), ('A', 6, 4), ('A', 10, 0), ('A', 6, 1)),
+        (),
+        (('A', 10, 6), ('R', 0, 0)),
+        (),
+        (('A', 10, 5), ('A', 10, 1), ('R', 1, 0), ('A', 10, 4), ('R', 2, 0), ('A', 10, 2), ('R', 2, 1), ('A', 10, 7), ('A', 10, 8)),
+        (('R', 4, 1),),
+        (),
+        (),
+        (('R', 6, 1), ('R', 5, 0), ('R', 7, 0), ('R', 7, 1)),
+    ),
+    (
+        (('A', 7, 5), ('A', 11, 0), ('A', 7, 2), ('A', 3, 1), ('A', 3, 0)),
+        (('A', 7, 1), ('A', 11, 2), ('A', 11, 5), ('A', 7, 0), ('A', 7, 4)),
+        (),
+        (('A', 11, 6),),
+        (('A', 11, 7), ('R', 1, 0), ('R', 1, 1), ('A', 11, 4)),
+        (('A', 11, 3), ('R', 3, 0), ('A', 11, 1), ('A', 11, 9), ('A', 11, 8)),
+        (),
+        (),
+        (('R', 5, 1), ('R', 5, 0), ('R', 7, 0), ('R', 7, 1)),
+    ),
+)
 
 
 def kernel(
@@ -31,7 +92,8 @@
     rows, slots, outs, layers, groups, fine = sizes
     far = 2 * W
     layer = lax.axis_index("layer")
-    group = lax.axis_index("row") * fine + lax.axis_index("col")
+    col = lax.axis_index("col")
+    group = lax.axis_index("row") * fine + col
     base = group * rows
     zero_at = rows * slots
     halo_at = zero_at + 1
@@ -87,16 +149,8 @@
         block = right[row * slots + slot]
         return jnp.where(hit > 0, block, jnp.zeros_like(block))
 
-    lists = [[] for _ in range(layers)]
-    for k, t in LOCAL_BELOW:
-        lists[k % layers].append((k, t))
+    lists, crossing = BELOW, LOCAL
     forwarded = {(rows + b, a) for a, b in FORWARD}
-    for n in range(layers):
-        k = rows + n
-        mine = [(k, t) for t in range(min(k - rows + W + 1, rows)) if (k, t) not in forwarded]
-        early = [(rows + a, b) for a, b in FORWARD if a == n]
-        lists[n] += early + [e for e in mine if e not in early]
-    crossing = [[e for e in LOCAL[n] if e not in LOCAL_BELOW] for n in range(layers)]
     down_most = max(len(x) for x in lists)
     cross_most = max(len(x) for x in crossing)
     lent_at = down_most + cross_most
@@ -162,17 +216,31 @@
             device_id=below, device_id_type=MESH,
         )
 
-    def part_copy(at, to):
-        return pltpu.make_async_remote_copy(
-            src_ref=part.at[at], dst_ref=recv.at[at], send_sem=part_send.at[at], recv_sem=part_recv.at[at],
+    def part_copy(at, recv_at, to):
+        return pltpu.make_async_remote_copy(
+            src_ref=part.at[at], dst_ref=recv.at[recv_at], send_sem=part_send.at[at], recv_sem=part_recv.at[recv_at],
             device_id={"layer": to}, device_id_type=MESH,
         )
 
     lx, ly = layer % 2, layer // 2
     flip_x, flip_y, both = ly * 2 + 1 - lx, (1 - ly) * 2 + lx, (1 - ly) * 2 + 1 - lx
 
-    def mates(row):
-        return (flip_x, flip_y) if X_FIRST[row] else (flip_y, flip_x)
+    def first_copy(row):
+        over_y = OVER_Y[row]
+        to = sel([n ^ 2 if over_y[n] else n ^ 1 for n in range(layers)])
+        return part_copy(row, sel([(3 if over_y[n] else 2) * rows + row for n in range(layers)]), to)
+
+    def x_copy(row):
+        return part_copy(rows + row, row, flip_x)
+
+    def y_copy(row):
+        return part_copy(2 * rows + row, rows + row, flip_y)
+
+    def x_direct(row):
+        return [n for n in range(layers) if not OVER_Y[row][n ^ 2]]
+
+    def y_direct(row):
+        return [n for n in range(layers) if OVER_Y[row][n ^ 1]]
 
     loads = [
         pltpu.make_async_copy(cols_hbm, cols_ref, load_sem.at[0]),
@@ -228,14 +296,17 @@
     cross_start(0)
     down_start(0)
 
-    @pl.when(has_above & (layer < 2))
-    def _():
-        target_copy().start()
-        for i in range(2):
-            @guard((0,) if i == 0 else (0, 1))
-            def _(i=i):
-                pack[lent_at + i] = block_of(W + i, rows + layers + layer)
-                lent_copy(i).start()
+    def lend_start(cond):
+        @pl.when(cond & has_above & (layer < 2))
+        def _():
+            target_copy().start()
+            for i in range(2):
+                @guard((0,) if i == 0 else (0, 1))
+                def _(i=i):
+                    pack[lent_at + i] = block_of(W + i, rows + layers + layer)
+                    lent_copy(i).start()
+
+    lend_start(col < fine - 1)
 
     for n in range(1, max(down_most, cross_most)):
         if n < cross_most:
@@ -248,7 +319,7 @@
     right[halo_at + far + layer] = block_of(layers + layer, rows + layer).T
 
     def arrive(k, t):
-        @guard((k % layers,), group < groups - 2 if t >= rows else has_above)
+        @pl.when(group < groups - 2 if t >= rows else has_above)
         def _():
             at = at_of(k, t)
             pltpu.make_async_remote_copy(
@@ -318,73 +389,77 @@
             return carry
         lax.fori_loop(0, outs, body, 0)
 
+    def settle(value, at, direct, copy):
+        if not direct:
+            kept[at - rows] = value
+        elif len(direct) == layers:
+            part[at] = value.astype(part.dtype)
+            copy().start()
+        else:
+            kept[at - rows] = value
+
+            @guard(direct)
+            def _():
+                part[at] = kept[at - rows].astype(part.dtype)
+                copy().start()
+
     def one_row(row):
-        first, second = mates(row)
-        part[2 * row + 1] = product(row, both).astype(part.dtype)
-        part_copy(2 * row + 1, first).start()
-        part[2 * row] = product(row, first).astype(part.dtype)
-        part_copy(2 * row, first).start()
-        kept[row] = product(row, second)
+        part[row] = product(row, both).astype(part.dtype)
+        first_copy(row).start()
+        settle(product(row, flip_x), rows + row, x_direct(row), lambda: x_copy(row))
+        settle(product(row, flip_y), 2 * rows + row, y_direct(row), lambda: y_copy(row))
         own[row] = product(row, layer)
 
-    def relay(row):
-        first, second = mates(row)
-        part_copy(2 * row + 1, first).wait_recv()
-        total = kept[row] + recv[2 * row + 1].astype(jnp.float32)
-        part[2 * rows + row] = total.astype(part.dtype)
-        part_copy(2 * rows + row, second).start()
-
-    needs = [[] for _ in range(rows + 2)]
-    for q in range(2):
+    def relay(row, over_y):
+        recv_at = (3 if over_y else 2) * rows + row
+        at = (1 if over_y else 2) * rows + row
+        part_copy(row, recv_at, flip_x).wait_recv()
+        total = kept[at - rows] + recv[recv_at].astype(jnp.float32)
+        part[at] = total.astype(part.dtype)
+        (x_copy(row) if over_y else y_copy(row)).start()
+
+    def lend(cond):
+        @pl.when(cond & has_below)
+        def _():
+            target_copy().wait_recv()
+            for i in range(2):
+                @guard((0,) if i == 0 else (0, 1))
+                def _(i=i):
+                    lent_copy(i).wait_recv()
+                    terms(i)
+
+    for row in range(rows + 1):
+        if row == FAR_LEND:
+            lend_start(col == fine - 1)
+        if row == FAR_TERMS:
+            for n in range(2):
+                @pl.when(layer == n)
+                def _():
+                    lend(col == 0)
         for n in range(layers):
-            k = q * layers + n
-            for t in range(max(0, k - rows + W + 1)):
-                if (t % layers) != n:
-                    needs[0 if k < rows - 1 and t < far - rows + 1 else 1].append((k, t))
-    fore = [(rows + a, b) for a, b in FORWARD]
-    needs[1] += fore
-    for n in range(layers):
-        k = rows + n
-        rest = [e for e in lists[n] if e[0] == k and e not in fore]
-        rest += [e for e in sorted(forwarded) if e[0] == k]
-        rest += [(k, t) for t in range(rows, k - rows + W + 1)]
-        needs[2 + n] += rest
-
-    relay_at = [[min(row + 2, rows) if row != 1 + n else 2 + n for row in range(rows)] for n in range(layers)]
-
-    for row in range(rows):
-        for at_row in range(rows):
-            which = [n for n in range(layers) if relay_at[n][at_row] == row]
-            if which:
-                guard(which)(functools.partial(relay, at_row))
-        if row == 2:
-            @pl.when(has_below & (layer < 2))
-            def _():
-                target_copy().wait_recv()
-                for i in range(2):
-                    @guard((0,) if i == 0 else (0, 1))
-                    def _(i=i):
-                        lent_copy(i).wait_recv()
-                        terms(i)
-        for k, t in needs[row]:
-            arrive(k, t)
+            @pl.when(layer == n)
+            def _(n=n):
+                for what, first, second in STEPS[n][row]:
+                    if what == "A":
+                        arrive(first, second)
+                    elif what == "R":
+                        relay(first, second)
+                    else:
+                        lend(col > 0)
+        if row == rows:
+            break
         if row >= W:
             @guard((0,) if row == W else (0, 1), has_above)
             def _(row=row):
                 for o in range(outs):
                     term_copy((row - W) * outs + o).wait_recv()
         one_row(row)
-    for at_row in range(rows):
-        which = [n for n in range(layers) if relay_at[n][at_row] >= rows]
-        if which:
-            guard(which)(functools.partial(relay, at_row))
 
     for row in range(rows):
-        first, second = mates(row)
-        part_copy(2 * row, first).wait_recv()
-        part_copy(2 * rows + row, second).wait_recv()
-        total = own[row] + recv[2 * row].astype(jnp.float32)
-        total = total + recv[2 * rows + row].astype(jnp.float32)
+        part_copy(row, row, flip_x).wait_recv()
+        part_copy(row, rows + row, flip_x).wait_recv()
+        total = own[row] + recv[row].astype(jnp.float32)
+        total = total + recv[rows + row].astype(jnp.float32)
         out_ref[row, 0] = total.astype(out_ref.dtype)
 
     for n in range(cross_most):
@@ -411,10 +486,9 @@
                     term_copy(i * outs + o).wait_send()
 
     for row in range(rows):
-        first, second = mates(row)
-        part_copy(2 * row, first).wait_send()
-        part_copy(2 * row + 1, first).wait_send()
-        part_copy(2 * rows + row, second).wait_send()
+        first_copy(row).wait_send()
+        x_copy(row).wait_send()
+        y_copy(row).wait_send()
 
 
 def solution(mesh):
@@ -430,7 +504,7 @@
         block = (size, size)
         halo = 3 * far
         sent = 3 * rows
-        packs = 20
+        packs = max(map(len, LOCAL)) + max(map(len, BELOW)) + 2
         return pl.pallas_call(
             functools.partial(kernel, (rows, slots, outs, layers, groups, fine)),
             out_shape=jax.ShapeDtypeStruct((rows, outs // layers) + block, jnp.bfloat16),
@@ -452,8 +526,8 @@
                 pltpu.VMEM((2 * outs,) + block, jnp.bfloat16),
                 pltpu.VMEM((sent,) + block, jnp.bfloat16),
                 pltpu.VMEM((rows,) + block, jnp.float32),
-                pltpu.VMEM((rows,) + block, jnp.float32),
-                pltpu.VMEM((sent,) + block, jnp.bfloat16),
+                pltpu.VMEM((2 * rows,) + block, jnp.float32),
+                pltpu.VMEM((4 * rows,) + block, jnp.bfloat16),
                 pltpu.SemaphoreType.DMA((3,)),
                 pltpu.SemaphoreType.DMA((packs,)),
                 pltpu.SemaphoreType.DMA((halo,)),
@@ -465,7 +539,7 @@
                 pltpu.SemaphoreType.DMA((2 * outs,)),
                 pltpu.SemaphoreType.DMA((2 * outs,)),
                 pltpu.SemaphoreType.DMA((sent,)),
-                pltpu.SemaphoreType.DMA((sent,)),
+                pltpu.SemaphoreType.DMA((4 * rows,)),
             ],
             compiler_params=pltpu.CompilerParams(collective_id=0, has_side_effects=True),
         )(cols.T, outcols.T, vals.reshape((rows * slots,) + block))

time: 66.3 us -> 59.2 us (0.89)
  Pallas kernels: 63.9 us -> 56.7 us
    pallas_call x1, Pallas kernels: 63.9 us -> 56.7 us  [per_device(): pl.pallas_call(functools.partial(kernel, (rows, slots, outs, layers, grou...]
where the time goes in v2:
time: 59.2 us; the launch traced here: 59 us
  Pallas kernels  56.7 us (96%)
  local copies, waits for them, and re-layouts  2.26 us (4%)
    pallas_call x1, Pallas kernels, per_device(): pl.pallas_call(functools.partial(kernel, (rows, slots, outs, layers, grou...  56.7 us
    unnamed x1, local copies, waits for them, and re-layouts  2.26 us

profile of v2, /device:TPU:0, one launch (start us, length us, event | category | flops | bytes accessed | tf_op | source)
XLA Modules:
  0.0 59.0 jit_solution(8708362272032450718)
XLA Ops:
  0.0 56.7 %shard_map.37 = bf16[8,1,256,256]{3,2,1,0:T(8,128)(2,1)} custom-call(s32[4,8]{1,0:T(4,128)} %bitcast.4, s32[4,8]{1,0:T(4,128)} %bitcast.5, bf16[32,256,256]{2,1,0:T(8,128)(2,1)} %bitcast.3), custom_call_target="tpu_custom_call" | custom-call | tf_op jit(solution)/shard_map/pallas_call | solution.py:508
  56.7 2.3 %copy.5 = bf16[8,1,256,256]{3,2,1,0:T(8,128)(2,1)} copy(bf16[8,1,256,256]{3,2,1,0:T(8,128)(2,1)} %shard_map.37) | data formatting | bytes 2097152

commit v3 on v2

--- a/solution.py
+++ b/solution.py
@@ -10,74 +10,173 @@
 W = 6
 MESH = pl.DeviceIdType.MESH
 
-FAR_LEND, FAR_TERMS = 2, 4
+FAR_LEND, FAR_TERMS = 1, 4
+UNITS = tuple((row, unit) for row in range(W) for unit in range(4)) + (
+    (6, 0), (6, 1), (6, 2), (7, 0), (7, 1), (7, 2), (6, 3), (7, 3),
+)
 LOCAL = (
-    ((2, 0), (6, 0), (7, 0), (5, 0)),
-    ((7, 5), (4, 1), (6, 1), (3, 1), (7, 1)),
-    ((5, 2), (7, 2), (4, 2)),
-    ((5, 3), (6, 3)),
+    ((5, 0), (6, 4), (2, 0), (7, 4)),
+    ((7, 5), (3, 1), (4, 1), (7, 1), (6, 1)),
+    ((4, 2), (5, 2), (7, 2)),
+    ((6, 3), (5, 3)),
 )
 BELOW = (
-    ((8, 5), (8, 1), (8, 0), (8, 4), (8, 6)),
-    ((9, 2), (9, 6), (9, 1), (9, 7), (9, 5), (9, 4), (9, 3)),
-    ((10, 3), (6, 4), (10, 0), (10, 6), (10, 5), (10, 4), (10, 2), (10, 7)),
-    ((11, 0), (3, 0), (11, 5), (7, 4), (11, 6), (11, 7), (11, 4), (11, 3)),
+    ((8, 4), (8, 1), (8, 0), (8, 2), (8, 6), (8, 5)),
+    ((9, 2), (9, 7), (9, 1), (9, 5), (9, 4), (9, 3), (9, 6)),
+    ((6, 0), (10, 3), (10, 5), (10, 1), (10, 6), (10, 2), (10, 7), (10, 4)),
+    ((11, 0), (3, 0), (7, 0), (11, 4), (11, 7), (11, 5), (11, 3), (11, 6)),
 )
-FORWARD = ((2, 0), (1, 3), (1, 2), (3, 0), (0, 1), (2, 3))
+FORWARD = ((1, 3), (0, 1), (3, 0), (2, 3), (0, 2))
 OVER_Y = (
     (0, 0, 1, 0),
-    (0, 1, 0, 0),
-    (1, 0, 1, 0),
-    (0, 0, 0, 1),
-    (1, 0, 1, 1),
-    (0, 1, 0, 0),
-    (1, 0, 1, 1),
+    (0, 1, 0, 1),
+    (1, 0, 0, 0),
+    (0, 0, 1, 1),
+    (0, 0, 1, 1),
     (1, 1, 0, 0),
+    (0, 1, 1, 1),
+    (1, 0, 0, 0),
 )
 STEPS = (
     (
-        (('A', 8, 5), ('A', 4, 1), ('A', 4, 2)),
-        (),
-        (('A', 8, 1), ('T', 0, 0), ('A', 8, 0), ('A', 8, 3), ('A', 8, 4), ('R', 0, 0), ('A', 8, 2), ('A', 8, 6)),
-        (),
-        (),
-        (('R', 0, 1),),
-        (('R', 2, 0), ('R', 2, 1)),
-        (('R', 3, 0), ('R', 4, 0), ('R', 4, 1)),
+        (('A', 4, 2), ('A', 8, 4), ('A', 4, 1)),
+        (),
+        (),
+        (),
+        (),
+        (),
+        (('A', 8, 1),),
+        (),
+        (('T', 0, 0), ('A', 8, 0), ('A', 8, 3), ('R', 0, 0), ('A', 8, 2), ('R', 0, 1), ('A', 8, 6), ('A', 8, 5)),
+        (),
+        (),
+        (('R', 2, 0),),
+        (),
+        (),
+        (),
+        (),
+        (),
+        (),
+        (),
+        (('R', 3, 1),),
+        (),
+        (),
+        (),
+        (),
+        (),
+        (('R', 3, 0),),
+        (),
+        (),
+        (('R', 4, 0), ('R', 4, 1)),
+        (),
+        (('R', 6, 1),),
+        (('R', 7, 0),),
+        (),
+    ),
+    (
+        (('A', 5, 0), ('A', 9, 2), ('A', 5, 3), ('A', 9, 7), ('A', 5, 2)),
+        (),
+        (),
+        (),
+        (),
+        (),
+        (('A', 9, 1), ('R', 0, 0)),
+        (),
+        (),
+        (),
+        (),
+        (),
+        (('A', 9, 5), ('R', 1, 0), ('T', 0, 0), ('A', 9, 4), ('R', 1, 1), ('A', 9, 0), ('A', 9, 3), ('A', 9, 6)),
+        (),
+        (),
+        (),
+        (('R', 3, 1),),
+        (),
+        (),
+        (),
+        (),
+        (),
+        (),
+        (),
+        (),
+        (),
+        (),
+        (('R', 3, 0), ('R', 4, 1)),
+        (),
+        (('R', 4, 0),),
+        (),
+        (),
         (('R', 6, 0), ('R', 6, 1)),
     ),
     (
-        (('A', 5, 3), ('A', 9, 2), ('A', 5, 2), ('A', 9, 6), ('A', 5, 0)),
-        (),
-        (('A', 9, 1), ('R', 0, 0), ('T', 0, 0)),
-        (('A', 9, 7), ('R', 1, 0), ('A', 9, 5), ('A', 9, 4), ('A', 9, 0), ('A', 9, 3)),
-        (),
-        (),
-        (('R', 3, 0), ('R', 3, 1)),
-        (('R', 4, 1), ('R', 5, 0)),
-        (('R', 6, 1),),
+        (('A', 6, 3), ('A', 6, 0), ('A', 6, 4), ('A', 10, 3), ('A', 2, 0), ('A', 10, 5), ('A', 6, 1)),
+        (),
+        (),
+        (),
+        (),
+        (('R', 0, 0),),
+        (('A', 10, 1),),
+        (),
+        (),
+        (),
+        (),
+        (),
+        (('A', 10, 6),),
+        (),
+        (),
+        (),
+        (('A', 10, 2), ('A', 10, 0), ('R', 2, 0), ('A', 10, 7), ('R', 2, 1), ('A', 10, 4), ('A', 10, 8)),
+        (),
+        (),
+        (),
+        (),
+        (),
+        (),
+        (),
+        (),
+        (),
+        (),
+        (),
+        (),
+        (),
+        (),
+        (),
+        (('R', 5, 1), ('R', 5, 0), ('R', 7, 0), ('R', 7, 1)),
     ),
     (
-        (('A', 2, 0), ('A', 10, 3), ('A', 6, 3), ('A', 6, 0), ('A', 6, 4), ('A', 10, 0), ('A', 6, 1)),
-        (),
-        (('A', 10, 6), ('R', 0, 0)),
-        (),
-        (('A', 10, 5), ('A', 10, 1), ('R', 1, 0), ('A', 10, 4), ('R', 2, 0), ('A', 10, 2), ('R', 2, 1), ('A', 10, 7), ('A', 10, 8)),
-        (('R', 4, 1),),
-        (),
-        (),
-        (('R', 6, 1), ('R', 5, 0), ('R', 7, 0), ('R', 7, 1)),
-    ),
-    (
-        (('A', 7, 5), ('A', 11, 0), ('A', 7, 2), ('A', 3, 1), ('A', 3, 0)),
-        (('A', 7, 1), ('A', 11, 2), ('A', 11, 5), ('A', 7, 0), ('A', 7, 4)),
-        (),
-        (('A', 11, 6),),
-        (('A', 11, 7), ('R', 1, 0), ('R', 1, 1), ('A', 11, 4)),
-        (('A', 11, 3), ('R', 3, 0), ('A', 11, 1), ('A', 11, 9), ('A', 11, 8)),
-        (),
-        (),
-        (('R', 5, 1), ('R', 5, 0), ('R', 7, 0), ('R', 7, 1)),
+        (('A', 7, 5), ('A', 11, 0), ('A', 3, 1), ('A', 3, 0), ('A', 7, 2)),
+        (),
+        (),
+        (),
+        (('A', 7, 1), ('A', 7, 0), ('A', 11, 2), ('A', 7, 4), ('A', 11, 4)),
+        (),
+        (),
+        (),
+        (),
+        (),
+        (('A', 11, 7),),
+        (),
+        (),
+        (),
+        (),
+        (),
+        (('A', 11, 5),),
+        (),
+        (),
+        (),
+        (('R', 1, 0), ('R', 1, 1), ('A', 11, 3), ('R', 2, 0), ('A', 11, 6), ('A', 11, 1), ('A', 11, 9), ('A', 11, 8)),
+        (),
+        (('R', 5, 1),),
+        (),
+        (),
+        (),
+        (),
+        (),
+        (),
+        (),
+        (),
+        (),
+        (('R', 5, 0), ('R', 6, 1), ('R', 7, 0)),
     ),
 )
 
@@ -336,7 +435,10 @@
                 def _():
                     pass_copy(passed.index((k, t))).start()
 
-    def product(row, o):
+    outputs = (both, flip_x, flip_y, layer)
+
+    def product(row, unit):
+        o = outputs[unit]
         target = targets_ref[o, row]
         there = target - base
         near = jnp.clip(there, 0, rows - 1)
@@ -360,7 +462,7 @@
             total = term if total is None else total + term
         if row >= W:
             lends = ((layer == 0) | ((layer == 1) & (row > W))) & has_above
-            theirs = terms_in[(row - W) * outs + o].astype(jnp.float32)
+            theirs = terms_in[(row - W) * outs + unit].astype(jnp.float32)
             total = total + jnp.where(lends, theirs, jnp.zeros_like(theirs))
         slot, hit = find(row, target)
         mine = (hit > 0) & (target >= 0)
@@ -368,26 +470,30 @@
         twice = jnp.where(mine, 2.0 * block, jnp.zeros_like(block))
         return twice - total
 
-    def terms(i):
-        def body(o, carry):
-            target = targets_up[o, W + i]
-            there = target - base
-            near = jnp.clip(there, 0, rows - 1)
-            slot, hit = find(near, base + layers + layer)
-            local_at = jnp.where(hit > 0, near * slots + slot, zero_at)
-            t = there - rows
-            reach = layers + layer >= t + rows - W
-            far_at = jnp.where(reach, halo_at + far + t, zero_at)
-            at = jnp.where(there < rows, local_at, far_at)
-            at = jnp.where((target >= 0) & (there >= 0), at, zero_at)
-            at = jnp.clip(at, 0, right.shape[0] - 1)
-            term = lax.dot_general(
-                lent[i], right[at], (((1,), (1,)), ((), ())), preferred_element_type=jnp.float32,
-            )
-            terms_out[i * outs + o] = term.astype(terms_out.dtype)
-            term_copy(i * outs + o).start()
-            return carry
-        lax.fori_loop(0, outs, body, 0)
+    def terms():
+        for row, unit in UNITS:
+            if row < W:
+                continue
+
+            @guard((0,) if row == W else (0, 1))
+            def _(row=row, unit=unit):
+                target = targets_up[outputs[unit], row]
+                there = target - base
+                near = jnp.clip(there, 0, rows - 1)
+                slot, hit = find(near, base + layers + layer)
+                local_at = jnp.where(hit > 0, near * slots + slot, zero_at)
+                t = there - rows
+                reach = layers + layer >= t + rows - W
+                far_at = jnp.where(reach, halo_at + far + t, zero_at)
+                at = jnp.where(there < rows, local_at, far_at)
+                at = jnp.where((target >= 0) & (there >= 0), at, zero_at)
+                at = jnp.clip(at, 0, right.shape[0] - 1)
+                term = lax.dot_general(
+                    lent[row - W], right[at], (((1,), (1,)), ((), ())), preferred_element_type=jnp.float32,
+                )
+                n = (row - W) * outs + unit
+                terms_out[n] = term.astype(terms_out.dtype)
+                term_copy(n).start()
 
     def settle(value, at, direct, copy):
         if not direct:
@@ -403,12 +509,21 @@
                 part[at] = kept[at - rows].astype(part.dtype)
                 copy().start()
 
-    def one_row(row):
-        part[row] = product(row, both).astype(part.dtype)
-        first_copy(row).start()
-        settle(product(row, flip_x), rows + row, x_direct(row), lambda: x_copy(row))
-        settle(product(row, flip_y), 2 * rows + row, y_direct(row), lambda: y_copy(row))
-        own[row] = product(row, layer)
+    def one(row, unit):
+        if row >= W:
+            @guard((0,) if row == W else (0, 1), has_above)
+            def _():
+                term_copy((row - W) * outs + unit).wait_recv()
+        value = product(row, unit)
+        if unit == 0:
+            part[row] = value.astype(part.dtype)
+            first_copy(row).start()
+        elif unit == 1:
+            settle(value, rows + row, x_direct(row), lambda: x_copy(row))
+        elif unit == 2:
+            settle(value, 2 * rows + row, y_direct(row), lambda: y_copy(row))
+        else:
+            own[row] = value
 
     def relay(row, over_y):
         recv_at = (3 if over_y else 2) * rows + row
@@ -423,37 +538,33 @@
         def _():
             target_copy().wait_recv()
             for i in range(2):
-                @guard((0,) if i == 0 else (0, 1))
-                def _(i=i):
-                    lent_copy(i).wait_recv()
-                    terms(i)
-
-    for row in range(rows + 1):
-        if row == FAR_LEND:
+                guard((0,) if i == 0 else (0, 1))(lambda i=i: lent_copy(i).wait_recv())
+            terms()
+
+    for step in range(len(UNITS) + 1):
+        row, unit = UNITS[step] if step < len(UNITS) else (rows, 0)
+        if (row, unit) == (FAR_LEND, 0):
             lend_start(col == fine - 1)
-        if row == FAR_TERMS:
+        if (row, unit) == (FAR_TERMS, 0):
             for n in range(2):
                 @pl.when(layer == n)
                 def _():
                     lend(col == 0)
         for n in range(layers):
+            if not STEPS[n][step]:
+                continue
+
             @pl.when(layer == n)
             def _(n=n):
-                for what, first, second in STEPS[n][row]:
+                for what, first, second in STEPS[n][step]:
                     if what == "A":
                         arrive(first, second)
                     elif what == "R":
                         relay(first, second)
                     else:
                         lend(col > 0)
-        if row == rows:
-            break
-        if row >= W:
-            @guard((0,) if row == W else (0, 1), has_above)
-            def _(row=row):
-                for o in range(outs):
-                    term_copy((row - W) * outs + o).wait_recv()
-        one_row(row)
+        if step < len(UNITS):
+            one(row, unit)
 
     for row in range(rows):
         part_copy(row, row, flip_x).wait_recv()
@@ -541,8 +652,14 @@
                 pltpu.SemaphoreType.DMA((sent,)),
                 pltpu.SemaphoreType.DMA((4 * rows,)),
             ],
-            compiler_params=pltpu.CompilerParams(collective_id=0, has_side_effects=True),
-        )(cols.T, outcols.T, vals.reshape((rows * slots,) + block))
+            compiler_params=pltpu.CompilerParams(
+                collective_id=0, has_side_effects=True, vmem_limit_bytes=52 * 2 ** 20,
+            ),
+        )(
+            pltpu.with_memory_space_constraint(cols.T, pltpu.HBM),
+            pltpu.with_memory_space_constraint(outcols.T, pltpu.HBM),
+            vals.reshape((rows * slots,) + block),
+        )
 
     in_specs = (
         P(("row", "col"), "layer"),

time: 59.2 us -> 54.8 us (0.926)
  Pallas kernels: 56.7 us -> 53.2 us
  local copies, waits for them, and re-layouts: 2.26 us -> 0.97 us
    pallas_call x1, Pallas kernels: 56.7 us -> 53.2 us  [per_device(): pl.pallas_call(functools.partial(kernel, (rows, slots, outs, layers, grou...]
    unnamed x1, local copies, waits for them, and re-layouts: 2.26 us -> 0.97 us
where the time goes in v3:
time: 54.8 us; the launch traced here: 54.2 us
  Pallas kernels  53.2 us (97%)
  local copies, waits for them, and re-layouts  0.97 us (2%)
    pallas_call x1, Pallas kernels, per_device(): pl.pallas_call(functools.partial(kernel, (rows, slots, outs, layers, grou...  53.2 us

profile of v3, /device:TPU:0, one launch (start us, length us, event | category | flops | bytes accessed | tf_op | source)
XLA Modules:
  0.0 54.2 jit_solution(2218297196681073154)
XLA Ops:
  0.0 53.2 %shard_map.37 = bf16[8,1,256,256]{3,2,1,0:T(8,128)(2,1)S(1)} custom-call(s32[4,8]{1,0:T(4,128)} %bitcast.4, s32[4,8]{1,0:T(4,128)} %bitcast.5, bf16[32,256,256]{2,1,0:T(8,128)(2,1)} %bitcast.3), custom_call_target="tpu_custom_call" | custom-call | tf_op jit(solution)/shard_map/pallas_call | solution.py:619
  53.2 1.0 %copy.5 = bf16[8,1,256,256]{3,2,1,0:T(8,128)(2,1)} copy(bf16[8,1,256,256]{3,2,1,0:T(8,128)(2,1)S(1)} %shard_map.37) | data formatting | bytes 2097152

commit v4 on v3

--- a/solution.py
+++ b/solution.py
@@ -10,14 +10,14 @@
 W = 6
 MESH = pl.DeviceIdType.MESH
 
-FAR_LEND, FAR_TERMS = 1, 4
+FAR_LEND, FAR_TERMS = 1, 5
 UNITS = tuple((row, unit) for row in range(W) for unit in range(4)) + (
     (6, 0), (6, 1), (6, 2), (7, 0), (7, 1), (7, 2), (6, 3), (7, 3),
 )
 LOCAL = (
     ((5, 0), (6, 4), (2, 0), (7, 4)),
     ((7, 5), (3, 1), (4, 1), (7, 1), (6, 1)),
-    ((4, 2), (5, 2), (7, 2)),
+    ((5, 2), (4, 2), (7, 2)),
     ((6, 3), (5, 3)),
 )
 BELOW = (
@@ -39,15 +39,15 @@
 )
 STEPS = (
     (
-        (('A', 4, 2), ('A', 8, 4), ('A', 4, 1)),
-        (),
-        (),
-        (),
-        (),
-        (),
-        (('A', 8, 1),),
-        (),
-        (('T', 0, 0), ('A', 8, 0), ('A', 8, 3), ('R', 0, 0), ('A', 8, 2), ('R', 0, 1), ('A', 8, 6), ('A', 8, 5)),
+        (('A', 8, 4), ('A', 4, 2), ('A', 4, 1)),
+        (),
+        (),
+        (),
+        (),
+        (),
+        (('A', 8, 1), ('A', 8, 0)),
+        (),
+        (('A', 8, 3), ('R', 0, 0), ('T', 0, 0), ('A', 8, 2), ('R', 0, 1), ('A', 8, 6), ('A', 8, 5)),
         (),
         (),
         (('R', 2, 0),),
@@ -61,10 +61,10 @@
         (('R', 3, 1),),
         (),
         (),
-        (),
-        (),
-        (),
         (('R', 3, 0),),
+        (),
+        (),
+        (),
         (),
         (),
         (('R', 4, 0), ('R', 4, 1)),
@@ -125,7 +125,7 @@
         (),
         (),
         (),
-        (('A', 10, 2), ('A', 10, 0), ('R', 2, 0), ('A', 10, 7), ('R', 2, 1), ('A', 10, 4), ('A', 10, 8)),
+        (('A', 10, 2), ('R', 2, 0), ('A', 10, 7), ('A', 10, 0), ('A', 10, 4), ('R', 2, 1), ('A', 10, 8)),
         (),
         (),
         (),
@@ -144,7 +144,7 @@
         (('R', 5, 1), ('R', 5, 0), ('R', 7, 0), ('R', 7, 1)),
     ),
     (
-        (('A', 7, 5), ('A', 11, 0), ('A', 3, 1), ('A', 3, 0), ('A', 7, 2)),
+        (('A', 7, 5), ('A', 11, 0), ('A', 3, 1), ('A', 7, 2), ('A', 3, 0)),
         (),
         (),
         (),

time: 54.8 us -> 54.8 us (level)
  no operation moved by 1% of the time
where the time goes in v4:
time: 54.8 us; the launch traced here: 54.4 us
  Pallas kernels  53.4 us (97%)
  local copies, waits for them, and re-layouts  0.97 us (2%)
    pallas_call x1, Pallas kernels, per_device(): pl.pallas_call(functools.partial(kernel, (rows, slots, outs, layers, grou...  53.4 us

profile of v4, /device:TPU:0, one launch (start us, length us, event | category | flops | bytes accessed | tf_op | source)
XLA Modules:
  0.0 54.4 jit_solution(2172818480104250942)
XLA Ops:
  0.0 53.4 %shard_map.37 = bf16[8,1,256,256]{3,2,1,0:T(8,128)(2,1)S(1)} custom-call(s32[4,8]{1,0:T(4,128)} %bitcast.4, s32[4,8]{1,0:T(4,128)} %bitcast.5, bf16[32,256,256]{2,1,0:T(8,128)(2,1)} %bitcast.3), custom_call_target="tpu_custom_call" | custom-call | tf_op jit(solution)/shard_map/pallas_call | solution.py:619
  53.4 1.0 %copy.5 = bf16[8,1,256,256]{3,2,1,0:T(8,128)(2,1)} copy(bf16[8,1,256,256]{3,2,1,0:T(8,128)(2,1)S(1)} %shard_map.37) | data formatting | bytes 2097152

commit v5 on v4

--- a/solution.py
+++ b/solution.py
@@ -69,8 +69,8 @@
         (),
         (('R', 4, 0), ('R', 4, 1)),
         (),
-        (('R', 6, 1),),
-        (('R', 7, 0),),
+        (('R', 7, 0), ('R', 6, 1)),
+        (),
         (),
     ),
     (
@@ -101,11 +101,11 @@
         (),
         (),
         (),
-        (('R', 3, 0), ('R', 4, 1)),
+        (('R', 3, 0),),
         (),
         (('R', 4, 0),),
         (),
-        (),
+        (('R', 4, 1),),
         (('R', 6, 0), ('R', 6, 1)),
     ),
     (
@@ -156,15 +156,15 @@
         (),
         (('A', 11, 7),),
         (),
-        (),
-        (),
-        (),
-        (),
+        (('R', 1, 1),),
+        (),
+        (),
+        (('R', 1, 0),),
         (('A', 11, 5),),
         (),
         (),
         (),
-        (('R', 1, 0), ('R', 1, 1), ('A', 11, 3), ('R', 2, 0), ('A', 11, 6), ('A', 11, 1), ('A', 11, 9), ('A', 11, 8)),
+        (('A', 11, 3), ('R', 2, 0), ('A', 11, 6), ('A', 11, 1), ('A', 11, 9), ('A', 11, 8)),
         (),
         (('R', 5, 1),),
         (),

time: 54.8 us -> 54.8 us (level)
  no operation moved by 1% of the time
where the time goes in v5:
time: 54.8 us; the launch traced here: 54.4 us
  Pallas kernels  53.4 us (97%)
  local copies, waits for them, and re-layouts  0.97 us (2%)
    pallas_call x1, Pallas kernels, per_device(): pl.pallas_call(functools.partial(kernel, (rows, slots, outs, layers, grou...  53.4 us

profile of v5, /device:TPU:0, one launch (start us, length us, event | category | flops | bytes accessed | tf_op | source)
XLA Modules:
  0.0 54.4 jit_solution(1231526468552426081)
XLA Ops:
  0.0 53.4 %shard_map.37 = bf16[8,1,256,256]{3,2,1,0:T(8,128)(2,1)S(1)} custom-call(s32[4,8]{1,0:T(4,128)} %bitcast.4, s32[4,8]{1,0:T(4,128)} %bitcast.5, bf16[32,256,256]{2,1,0:T(8,128)(2,1)} %bitcast.3), custom_call_target="tpu_custom_call" | custom-call | tf_op jit(solution)/shard_map/pallas_call | solution.py:619
  53.4 1.0 %copy.5 = bf16[8,1,256,256]{3,2,1,0:T(8,128)(2,1)} copy(bf16[8,1,256,256]{3,2,1,0:T(8,128)(2,1)S(1)} %shard_map.37) | data formatting | bytes 2097152
